TPU v7x, 32 devices: a whole 2x2x4 slice. The times are simulated.
32 devices in a mesh: shard: 4 (over y, core), ctx: 2 (over x), tp: 4 (over z).
Axes of the slice: x: 2, y: 2, z: 4, core: 2. Of those that a mesh axis runs over, the one named last changes fastest.
Arguments:
- tokens: bfloat16 [4, 1500, 768], P('shard', 'ctx'), may hold values from -8 to 8
- w_qkv: bfloat16 [768, 3, 768], P('shard', None, 'tp'), may hold values from -2 to 2
- b_qv: bfloat16 [2, 768], P(None, ('tp', 'shard')), may hold values from -3 to 3
- w_out: bfloat16 [768, 768], P('tp', 'shard'), may hold values from -1.5 to 1.5
- b_out: bfloat16 [768], P('shard'), may hold values from -2 to 2
- w_fc1: bfloat16 [768, 3072], P('shard', 'tp'), may hold values from -0.21875 to 0.21875
- b_fc1: bfloat16 [3072], P(('tp', 'shard')), may hold values from -3 to 3
- w_fc2: bfloat16 [3072, 768], P('tp', 'shard'), may hold values from -0.109375 to 0.109375
- b_fc2: bfloat16 [768], P('shard'), may hold values from -2 to 2
- ln1_gain: bfloat16 [768], P('shard'), may hold values from 0.25 to 1.75
- ln1_bias: bfloat16 [768], P('shard'), may hold values from -2 to 2
- ln2_gain: bfloat16 [768], P('shard'), may hold values from 0.25 to 1.75
- ln2_bias: bfloat16 [768], P('shard'), may hold values from -2 to 2
- cotangent: bfloat16 [4, 1500, 768], P('shard', 'ctx'), may hold values from -6 to 6
Outputs:
- output: bfloat16 [4, 1500, 768], P('shard', 'ctx')
- grad_tokens: bfloat16 [4, 1500, 768], P('shard', 'ctx')
- grad_w_qkv: float32 [768, 3, 768], P('shard', None, 'tp')
- grad_b_qv: float32 [2, 768], P(None, ('tp', 'shard'))
- grad_w_out: float32 [768, 768], P('tp', 'shard')
- grad_b_out: float32 [768], P('shard')
- grad_w_fc1: float32 [768, 3072], P('shard', 'tp')
- grad_b_fc1: float32 [3072], P(('tp', 'shard'))
- grad_w_fc2: float32 [3072, 768], P('tp', 'shard')
- grad_b_fc2: float32 [768], P('shard')
- grad_ln1_gain: float32 [768], P('shard')
- grad_ln1_bias: float32 [768], P('shard')
- grad_ln2_gain: float32 [768], P('shard')
- grad_ln2_bias: float32 [768], P('shard')
All inputs are finite; a program needn't handle non-finite values.
Results may differ from a plain program's by a relative error of at most 0.024.
Values may be sent and summed in bfloat16 or wider, within the bound.
No kernel may reach another device: no remote copies, remote signals or barrier semaphores. Data moves between devices by JAX's collectives and lax.ppermute only.
A program may use at most 128 MiB of HBM per device.

v0:
```python
import jax
import jax.numpy as jnp
from jax import lax
from jax.sharding import PartitionSpec as P

HEAD_DIM = 64


def norm_rows(rows, gain_vec, bias_vec):
    row_mean = jnp.mean(rows, axis=-1, keepdims=True)
    centred = rows - row_mean
    variance = jnp.mean(centred * centred, axis=-1, keepdims=True)
    return centred * lax.rsqrt(variance + 1e-05) * gain_vec + bias_vec


def exact_gelu(rows):
    return jax.nn.gelu(rows, approximate=False)


def split_heads(tensor):
    return tensor.reshape(
        tensor.shape[0], tensor.shape[1], tensor.shape[2] // HEAD_DIM, HEAD_DIM
    ).transpose(2, 0, 1, 3)


def join_heads(tensor):
    return tensor.transpose(1, 2, 0, 3).reshape(
        tensor.shape[1], tensor.shape[2], tensor.shape[0] * tensor.shape[3]
    )


def tensor_sum(partial_rows):
    return lax.psum(partial_rows.astype(jnp.bfloat16), "tp").astype(jnp.float32)


def head_forward(operands):
    queries, all_keys, values = operands
    scores = (
        jnp.einsum("cfd,cgd->cfg", queries, all_keys, preferred_element_type=jnp.float32) * 0.125
    )
    row_max = jnp.max(scores, axis=-1, keepdims=True)
    exponent = jnp.exp(scores - row_max)
    row_total = jnp.sum(exponent, axis=-1, keepdims=True)
    probabilities = (exponent / row_total).astype(jnp.bfloat16)
    head_out = jnp.einsum("cfg,cgd->cfd", probabilities, values, preferred_element_type=jnp.float32)
    return (head_out, (row_max + jnp.log(row_total))[..., 0])


def head_backward(operands):
    queries, all_keys, values, grad_out, logsum = operands
    scores = (
        jnp.einsum("cfd,cgd->cfg", queries, all_keys, preferred_element_type=jnp.float32) * 0.125
    )
    probabilities = jnp.exp(scores - logsum[..., None])
    grad_values = jnp.einsum(
        "cfg,cfd->cgd",
        probabilities.astype(jnp.bfloat16),
        grad_out,
        preferred_element_type=jnp.float32,
    )
    grad_probs = jnp.einsum("cfd,cgd->cfg", grad_out, values, preferred_element_type=jnp.float32)
    row_delta = jnp.sum(probabilities * grad_probs, axis=-1, keepdims=True)
    grad_scores = (probabilities * (grad_probs - row_delta)).astype(jnp.bfloat16)
    grad_queries = (
        jnp.einsum("cfg,cgd->cfd", grad_scores, all_keys, preferred_element_type=jnp.float32)
        * 0.125
    )
    grad_keys = (
        jnp.einsum("cfg,cfd->cgd", grad_scores, queries, preferred_element_type=jnp.float32) * 0.125
    )
    return (grad_queries, grad_keys, grad_values)


def per_device(
    tokens,
    w_qkv,
    b_qv,
    w_out,
    b_out,
    w_fc1,
    b_fc1,
    w_fc2,
    b_fc2,
    ln1_gain,
    ln1_bias,
    ln2_gain,
    ln2_bias,
    cotangent,
):
    vectors = jnp.stack([ln1_gain, ln1_bias, b_out, ln2_gain, ln2_bias, b_fc2], axis=1)
    qv_columns = b_qv.T
    fc1_columns = b_fc1[:, None]
    gathered = (
        lax.all_gather(w_qkv, "shard", axis=0, tiled=True),
        lax.all_gather(qv_columns, "shard", axis=0, tiled=True),
        lax.all_gather(vectors, "shard", axis=0, tiled=True),
        lax.all_gather(w_out, "shard", axis=1, tiled=True),
        lax.all_gather(w_fc1, "shard", axis=0, tiled=True),
        lax.all_gather(fc1_columns, "shard", axis=0, tiled=True),
        lax.all_gather(w_fc2, "shard", axis=1, tiled=True),
    )
    full_qkv, full_qv, full_vectors, full_out, full_fc1, full_fc1_bias, full_fc2 = gathered
    vector_table = full_vectors.astype(jnp.float32)
    gain_one = vector_table[:, 0]
    bias_one = vector_table[:, 1]
    out_bias = vector_table[:, 2]
    gain_two = vector_table[:, 3]
    bias_two = vector_table[:, 4]
    fc2_bias = vector_table[:, 5]
    inputs = tokens.astype(jnp.float32)
    normed_one = norm_rows(inputs, gain_one, bias_one).astype(jnp.bfloat16)
    projected = jnp.einsum(
        "cfd,dtk->cftk", normed_one, full_qkv, preferred_element_type=jnp.float32
    )
    qv_table = full_qv.astype(jnp.float32)
    bias_table = jnp.stack([qv_table[:, 0], jnp.zeros_like(qv_table[:, 0]), qv_table[:, 1]], axis=0)
    projected = (projected + bias_table).astype(jnp.bfloat16)
    queries = projected[:, :, 0]
    all_keys, all_values = (
        lax.all_gather(projected[:, :, 1], "ctx", axis=1, tiled=True),
        lax.all_gather(projected[:, :, 2], "ctx", axis=1, tiled=True),
    )
    split_queries = split_heads(queries)
    split_keys = split_heads(all_keys)
    split_values = split_heads(all_values)
    heads_out, logsum = lax.map(head_forward, (split_queries, split_keys, split_values))
    attended = join_heads(heads_out).astype(jnp.bfloat16)
    attn_part = jnp.einsum("cfk,kd->cfd", attended, full_out, preferred_element_type=jnp.float32)
    attn_sum = tensor_sum(attn_part)
    middle = inputs + (attn_sum + out_bias)
    normed_two = norm_rows(middle, gain_two, bias_two).astype(jnp.bfloat16)
    hidden_pre = jnp.einsum(
        "cfd,dh->cfh", normed_two, full_fc1, preferred_element_type=jnp.float32
    ) + full_fc1_bias[:, 0].astype(jnp.float32)
    activated = exact_gelu(hidden_pre).astype(jnp.bfloat16)
    mlp_part = jnp.einsum("cfh,hd->cfd", activated, full_fc2, preferred_element_type=jnp.float32)
    mlp_sum = tensor_sum(mlp_part)
    output = (middle + (mlp_sum + fc2_bias)).astype(jnp.bfloat16)
    regathered = (
        lax.all_gather(w_qkv, "shard", axis=0, tiled=True),
        lax.all_gather(w_out, "shard", axis=1, tiled=True),
        lax.all_gather(w_fc1, "shard", axis=0, tiled=True),
        lax.all_gather(w_fc2, "shard", axis=1, tiled=True),
    )
    full_qkv, full_out, full_fc1, full_fc2 = regathered
    grad_result = cotangent.astype(jnp.float32)
    grad_fc2 = jnp.einsum("cfh,cfd->hd", activated, cotangent, preferred_element_type=jnp.float32)
    grad_act = jnp.einsum("cfd,hd->cfh", cotangent, full_fc2, preferred_element_type=jnp.float32)
    unused_act, gelu_pull = jax.vjp(exact_gelu, hidden_pre)
    grad_pre = gelu_pull(grad_act)[0].astype(jnp.bfloat16)
    grad_fc1 = jnp.einsum("cfd,cfh->dh", normed_two, grad_pre, preferred_element_type=jnp.float32)
    grad_fc1_bias = jnp.sum(grad_pre.astype(jnp.float32), axis=(0, 1))
    grad_two_part = jnp.einsum(
        "cfh,dh->cfd", grad_pre, full_fc1, preferred_element_type=jnp.float32
    )
    grad_fc2_bias = jnp.sum(grad_result, axis=(0, 1))
    grad_normed_two = tensor_sum(grad_two_part)
    unused_two, pull_two = jax.vjp(norm_rows, middle, gain_two, bias_two)
    grad_mid_norm, grad_gain_two, grad_bias_two = pull_two(grad_normed_two)
    grad_middle = grad_result + grad_mid_norm
    grad_branch = grad_middle.astype(jnp.bfloat16)
    grad_out_bias = jnp.sum(grad_branch.astype(jnp.float32), axis=(0, 1))
    grad_out_w = jnp.einsum(
        "cfk,cfd->kd", attended, grad_branch, preferred_element_type=jnp.float32
    )
    grad_attended = jnp.einsum(
        "cfd,kd->cfk", grad_branch, full_out, preferred_element_type=jnp.float32
    ).astype(jnp.bfloat16)
    head_queries, head_keys, head_values = lax.map(
        head_backward, (split_queries, split_keys, split_values, split_heads(grad_attended), logsum)
    )
    grad_keys, grad_values = (
        lax.psum_scatter(
            join_heads(head_keys).astype(jnp.bfloat16), "ctx", scatter_dimension=1, tiled=True
        ).astype(jnp.float32),
        lax.psum_scatter(
            join_heads(head_values).astype(jnp.bfloat16), "ctx", scatter_dimension=1, tiled=True
        ).astype(jnp.float32),
    )
    grad_projected = jnp.stack([join_heads(head_queries), grad_keys, grad_values], axis=2).astype(
        jnp.bfloat16
    )
    grad_slots = jnp.sum(grad_projected.astype(jnp.float32), axis=(0, 1))
    grad_qv_columns = jnp.stack([grad_slots[0], grad_slots[2]], axis=1)
    grad_qkv_w = jnp.einsum(
        "cfd,cftk->dtk", normed_one, grad_projected, preferred_element_type=jnp.float32
    )
    grad_one_part = jnp.einsum(
        "cftk,dtk->cfd", grad_projected, full_qkv, preferred_element_type=jnp.float32
    )
    grad_normed_one = tensor_sum(grad_one_part)
    unused_one, pull_one = jax.vjp(norm_rows, inputs, gain_one, bias_one)
    grad_in_norm, grad_gain_one, grad_bias_one = pull_one(grad_normed_one)
    grad_tokens = (grad_middle + grad_in_norm).astype(jnp.bfloat16)
    grad_vectors = jnp.stack(
        [grad_gain_one, grad_bias_one, grad_out_bias, grad_gain_two, grad_bias_two, grad_fc2_bias],
        axis=1,
    )
    grad_tuple = (
        grad_qkv_w,
        grad_qv_columns,
        grad_vectors,
        grad_out_w,
        grad_fc1,
        grad_fc1_bias[:, None],
        grad_fc2,
    )
    grad_tuple = (
        lax.psum(grad_tuple[0].astype(jnp.bfloat16), "ctx").astype(jnp.float32),
        lax.psum(grad_tuple[1].astype(jnp.bfloat16), "ctx").astype(jnp.float32),
        lax.psum(grad_tuple[2].astype(jnp.bfloat16), "ctx").astype(jnp.float32),
        lax.psum(grad_tuple[3].astype(jnp.bfloat16), "ctx").astype(jnp.float32),
        lax.psum(grad_tuple[4].astype(jnp.bfloat16), "ctx").astype(jnp.float32),
        lax.psum(grad_tuple[5].astype(jnp.bfloat16), "ctx").astype(jnp.float32),
        lax.psum(grad_tuple[6].astype(jnp.bfloat16), "ctx").astype(jnp.float32),
    )
    grad_slices = (
        lax.psum_scatter(
            grad_tuple[0].astype(jnp.bfloat16), "shard", scatter_dimension=0, tiled=True
        ).astype(jnp.float32),
        lax.psum_scatter(
            grad_tuple[1].astype(jnp.bfloat16), "shard", scatter_dimension=0, tiled=True
        ).astype(jnp.float32),
        lax.psum_scatter(
            grad_tuple[2].astype(jnp.bfloat16), "shard", scatter_dimension=0, tiled=True
        ).astype(jnp.float32),
        lax.psum_scatter(
            grad_tuple[3].astype(jnp.bfloat16), "shard", scatter_dimension=1, tiled=True
        ).astype(jnp.float32),
        lax.psum_scatter(
            grad_tuple[4].astype(jnp.bfloat16), "shard", scatter_dimension=0, tiled=True
        ).astype(jnp.float32),
        lax.psum_scatter(
            grad_tuple[5].astype(jnp.bfloat16), "shard", scatter_dimension=0, tiled=True
        ).astype(jnp.float32),
        lax.psum_scatter(
            grad_tuple[6].astype(jnp.bfloat16), "shard", scatter_dimension=1, tiled=True
        ).astype(jnp.float32),
    )
    slice_qkv, slice_qv, slice_vectors, slice_out, slice_fc1, slice_fc1_bias, slice_fc2 = (
        grad_slices
    )
    return (
        output,
        grad_tokens,
        slice_qkv,
        slice_qv.T,
        slice_out,
        slice_vectors[:, 2],
        slice_fc1,
        slice_fc1_bias[:, 0],
        slice_fc2,
        slice_vectors[:, 5],
        slice_vectors[:, 0],
        slice_vectors[:, 1],
        slice_vectors[:, 3],
        slice_vectors[:, 4],
    )


def solution(mesh):
    placed = (
        P("shard", "ctx", None),
        P("shard", None, "tp"),
        P(None, ("tp", "shard")),
        P("tp", "shard"),
        P("shard"),
        P("shard", "tp"),
        P(("tp", "shard")),
        P("tp", "shard"),
        P("shard"),
        P("shard"),
        P("shard"),
        P("shard"),
        P("shard"),
        P("shard", "ctx", None),
    )
    return jax.shard_map(
        per_device,
        mesh=mesh,
        in_specs=placed,
        out_specs=(
            P("shard", "ctx", None),
            P("shard", "ctx", None),
            P("shard", None, "tp"),
            P(None, ("tp", "shard")),
            P("tp", "shard"),
            P("shard"),
            P("shard", "tp"),
            P(("tp", "shard")),
            P("tp", "shard"),
            P("shard"),
            P("shard"),
            P("shard"),
            P("shard"),
            P("shard"),
        ),
        check_vma=False,
    )
```

profile of v0, /device:TPU:0, one launch (start us, length us, event | category | flops | bytes accessed | tf_op | source)
XLA Modules:
  0.0 549.9 jit_solution(6944061020995750979)
XLA Ops:
  12.1 6.2 %all-gather.4 = bf16[4,48,2]{1,2,0:T(2,128)(2,1)S(1)} all-gather(bf16[1,48,2]{1,2,0:T(2,128)(2,1)} %bitcast.239), channel_id=1, replica_groups=mesh['shard'=4,'ctx'=2,'tp'=4] {'shard'}, dimensions={0}, use_global_device_ids=true | all-gather | bytes 960 | tf_op jit(solution)/shard_map/all_gather | solution.py:95
  21.7 5.5 all-gather.3
  28.0 7.1 %all_gather.36 = bf16[192,768]{0,1:T(8,128)(2,1)} all-gather(bf16[192,192]{0,1:T(8,128)(2,1)S(1)} %copy.88), channel_id=1, replica_groups=mesh['shard'=4,'ctx'=2,'tp'=4] {'shard'}, dimensions={1}, use_global_device_ids=true | all-gather | bytes 368640 | tf_op jit(solution)/shard_map/all_gather | solution.py:97
  35.4 13.1 %all_gather.32 = bf16[768,3,192]{2,1,0:T(4,128)(2,1)S(1)} all-gather(bf16[192,3,192]{2,1,0:T(4,128)(2,1)S(1)} %copy.78), channel_id=1, replica_groups=mesh['shard'=4,'ctx'=2,'tp'=4] {'shard'}, dimensions={0}, use_global_device_ids=true | all-gather | bytes 1105920 | tf_op jit(solution)/shard_map/all_gather | solution.py:94
  55.9 20.3 %all-gather.1 = bf16[1,1500,1,192]{3,2,0,1:T(2,128)(2,1)S(1)} all-gather(bf16[1,750,1,192]{3,2,0,1:T(2,128)(2,1)} %copy.84), channel_id=3, replica_groups=mesh['shard'=4,'ctx'=2,'tp'=4] {'ctx'}, dimensions={1}, use_global_device_ids=true | all-gather | bytes 864000 | tf_op jit(solution)/shard_map/all_gather | solution.py:121
  76.2 3.0 copy.85
  79.2 2.3 copy.87
  81.5 2.9 copy.82
  84.4 19.4 %all-gather = bf16[1,1500,1,192]{3,2,0,1:T(2,128)(2,1)S(1)} all-gather(bf16[1,750,1,192]{3,2,0,1:T(2,128)(2,1)} %copy.82), channel_id=2, replica_groups=mesh['shard'=4,'ctx'=2,'tp'=4] {'ctx'}, dimensions={1}, use_global_device_ids=true | all-gather | bytes 864000 | tf_op jit(solution)/shard_map/all_gather | solution.py:120
  103.8 3.0 copy.83
  109.4 14.3 %while.26 = (s32[]{:T(128)}, bf16[3,1,750,64]{2,3,1,0:T(8,128)(2,1)}, f32[3,1,750]{2,1,0:T(1,128)S(1)}, bf16[3,1,750,64]{3,2,1,0:T(8,128)(2,1)S(1)}, bf16[3,1,15...) while((s32[]{:T(128)}, bf16[3,1,750,64]{2,3,1,0:T(8,128)(2,1)}, ...), condition=%wide.region_5.6_spmd, body=%wide.region_2.5_spmd.sunk | while | flops 298124256 | bytes 17119008 | solution.py:126
  111.2 2.2 fusion.132
  123.7 2.7 fusion.66
  129.2 5.8 %all-reduce = bf16[768]{0:T(1024)(128)(2,1)S(1)} all-reduce(bf16[768]{0:T(1024)(128)(2,1)S(1)} %dynamic-update-slice), channel_id=4, replica_groups=mesh['shard'=4,'ctx'=2,'tp'=4] {'shard'}, use_global_device_ids=true, to_apply=%add | all-reduce | flops 768 | bytes 3072
  135.0 48.6 %all-reduce.13.cloned.1.call-done = bf16[1,750,768]{2,1,0:T(8,128)(2,1)} async-done(((bf16[1,750,768]{2,1,0:T(8,128)(2,1)}), bf16[1,750,768]{2,1,0:T(8,128)(2,1)}) %all-reduce.13.cloned.1.call-update) | async-done | bytes 1152016 | tf_op jit(solution)/shard_map/psum | solution.py:33
  186.1 9.1 %multiply_convert_fusion.1 = (bf16[750,768]{1,0:T(8,128)(2,1)}, f32[750,768]{1,0:T(8,128)}, f32[750,768]{1,0:T(8,128)}) fusion(f32[768]{0:T(1024)S(1)} %convert_element_type.289, bf16[768,768]{1,0:T(8,128)(2,1)} %all-gather.8.cloned.1.call-done, f32[768]{0:T(1024)S(1)} %get-tuple-element.136, f32[768]{0:T(1024)S(1)} %get-tuple-element.137, ...), kind=kOutput, calls=%fused_computation.83 | convolution fusion | flops 927936000 | bytes 9261936 | tf_op jit(solution)/shard_map/cfd,dh->cfh/dot_general | solution.py:132
  195.3 4.8 fusion.98
  203.3 55.2 %all-reduce.15.cloned.1.call-done = bf16[1,750,768]{2,1,0:T(8,128)(2,1)} async-done(((bf16[1,750,768]{2,1,0:T(8,128)(2,1)}), bf16[1,750,768]{2,1,0:T(8,128)(2,1)}) %all-reduce.15.cloned.1.call-update) | async-done | bytes 1152016 | tf_op jit(solution)/shard_map/psum | solution.py:33
  258.5 2.3 fusion.50
  269.4 25.9 %while.27 = (s32[]{:T(128)}, bf16[3,1,750,64]{2,3,1,0:T(8,128)(2,1)}, bf16[3,1,1500,64]{2,3,1,0:T(8,128)(2,1)}, bf16[3,1,1500,64]{2,3,1,0:T(8,128)(2,1)}, bf16[3...) while((s32[]{:T(128)}, ...), condition=%wide.region_15.16_spmd, body=%wide.region_13.15_spmd.sunk | while | flops 729143232 | bytes 49712548 | solution.py:169
  296.7 3.8 fusion.67
  300.5 37.4 %all-reduce.21.cloned.1.call-done = (bf16[1,1500,192]{1,2,0:T(8,128)(2,1)}, bf16[1,1500,192]{1,2,0:T(8,128)(2,1)}) async-done(((bf16[1,1500,192]{1,2,0:T(8,128)(2,1)}, bf16[1,1500,192]{1,2,0:T(8,128)(2,1)}), (bf16[1,1500,192]{1,2,0:T(8,128)(2,1)}, bf16[1,1500,192]{1,2,0:T(8,128)(2,1)})) %all-reduce.21.cloned.1.call-update) | async-done | bytes 1152016
  351.0 3.8 convolution_convert_fusion
  354.9 3.9 convolution_convert_fusion.1
  358.9 2.5 convolution_convert_fusion.2
  361.5 75.2 %all-reduce.17.cloned.1.call-done = (bf16[1,750,768]{2,1,0:T(8,128)(2,1)}, bf16[1,750,768]{2,1,0:T(8,128)(2,1)}) async-done(((bf16[1,750,768]{2,1,0:T(8,128)(2,1)}, bf16[1,750,768]{2,1,0:T(8,128)(2,1)}), (bf16[1,750,768]{2,1,0:T(8,128)(2,1)}, bf16[1,750,768]{2,1,0:T(8,128)(2,1)})) %all-reduce.17.cloned.1.call-update) | async-done | bytes 2304016 | tf_op jit(solution)/shard_map/psum | solution.py:33
  445.9 22.6 %reduce-scatter.20.cloned.1.call-done = bf16[192,768]{1,0:T(8,128)(2,1)} async-done(((bf16[768,768]{1,0:T(8,128)(2,1)}), bf16[192,768]{1,0:T(8,128)(2,1)}) %reduce-scatter.20.cloned.1.call-update) | async-done | bytes 294928 | tf_op jit(solution)/shard_map/reduce_scatter | solution.py:230
  468.5 28.0 %reduce-scatter.18.cloned.1.call-done = bf16[192,3,192]{2,0,1:T(8,128)(2,1)} async-done(((bf16[768,3,192]{2,0,1:T(8,128)(2,1)}), bf16[192,3,192]{2,0,1:T(8,128)(2,1)}) %reduce-scatter.18.cloned.1.call-update) | async-done | bytes 221200 | tf_op jit(solution)/shard_map/reduce_scatter | solution.py:218
  496.6 4.8 add_convert_fusion
  501.4 17.9 %reduce-scatter.28.cloned.1.call-done = bf16[192,6]{1,0:T(8,128)(2,1)} async-done(((bf16[768,6]{1,0:T(8,128)(2,1)}), bf16[192,6]{1,0:T(8,128)(2,1)}) %reduce-scatter.28.cloned.1.call-update) | async-done | bytes 2320
  520.1 5.1 all-reduce.4
  526.9 8.6 %all-reduce.19.cloned.1.call-done = (bf16[192,3,192]{2,0,1:T(8,128)(2,1)}, bf16[192,192]{1,0:T(8,128)(2,1)}, bf16[192,768]{1,0:T(8,128)(2,1)}, bf16[768,192]{0,1:T(8,128)(2,1)}) async-done(((bf16[192,3,192]{2,0,1:T(8,128)(2,1)}, bf16[192,192]{1,0:T(8,128)(2,1)}, bf16[192,768]{1,0:T(8,128)(2,1)}, bf16[768,192]{0,1:T(8,128)(2,1)}), (bf16[192,3,192]{2,0,1:T(8,128)(2,1)}, bf16[192,192]{1,0:T(8,128)(2,1)}, ...) | async-done | bytes 884752 | tf_op jit(solution)/shard_map/psum | solution.py:209
  (263 shorter events, 105.1 us)
Async XLA Ops:
  8.0 19.9 %copy-start.27 = (bf16[192,192]{1,0:T(8,128)(2,1)S(1)}, bf16[192,192]{1,0:T(8,128)(2,1)}, u32[]{:S(2)}) copy-start(bf16[192,192]{1,0:T(8,128)(2,1)} %param.21) | copy-start | bytes 221188
  8.0 27.1 %copy-start.22 = (bf16[192,3,192]{2,0,1:T(8,128)(2,1)S(1)}, bf16[192,3,192]{2,0,1:T(8,128)(2,1)}, u32[]{:S(2)}) copy-start(bf16[192,3,192]{2,0,1:T(8,128)(2,1)} %param.19) | copy-start | bytes 663556
  8.0 175.6 %all-reduce.13.cloned.1.call-start = ((), (), s32[]{:S(2)}) async-start(), calls=%async_computation.7 | async-start | bytes 2310144 | tf_op jit(solution)/shard_map/psum | solution.py:33
  21.7 5.5 %copy-start.28 = (f32[750]{0:T(1024)}, f32[750]{0:T(1024)S(1)}, u32[]{:S(2)}) copy-start(f32[750]{0:T(1024)S(1)} %fusion.53) | copy-start | bytes 9004
  27.9 158.2 %copy-start.31 = (f32[768]{0:T(1024)}, f32[768]{0:T(1024)S(1)}, u32[]{:S(2)}) copy-start(f32[768]{0:T(1024)S(1)} %get-tuple-element.136) | copy-start | bytes 9220
  35.4 15.3 %copy-start = (bf16[1,750,768]{2,1,0:T(8,128)(2,1)S(1)}, bf16[1,750,768]{2,1,0:T(8,128)(2,1)}, u32[]{:S(2)}) copy-start(bf16[1,750,768]{2,1,0:T(8,128)(2,1)} %param.18) | copy-start | bytes 3456004
  109.4 14.3 %copy-start.9 = (bf16[192,768]{0,1:T(8,128)(2,1)S(1)}, bf16[192,768]{0,1:T(8,128)(2,1)}, u32[]{:S(2)}) copy-start(bf16[192,768]{0,1:T(8,128)(2,1)} %all_gather.36) | copy-start | bytes 884740
  123.7 11.3 %copy-start.2 = (bf16[3,1,750,64]{3,2,1,0:T(8,128)(2,1)}, bf16[3,1,750,64]{3,2,1,0:T(8,128)(2,1)S(1)}, u32[]{:S(2)}) copy-start(bf16[3,1,750,64]{3,2,1,0:T(8,128)(2,1)S(1)} %get-tuple-element.396) | copy-start | bytes 864004
  123.7 5.2 copy-start.34
  126.4 59.7 %all-gather.8.cloned.1.call-start = ((), (), s32[]{:S(2)}) async-start(), calls=%async_computation.8 | async-start | bytes 1474560 | tf_op jit(solution)/shard_map/all_gather | solution.py:98
  127.0 68.2 %all-gather.10.cloned.1.call-start = ((), (), s32[]{:S(2)}) async-start(), calls=%async_computation.9 | async-start | bytes 1474560 | tf_op jit(solution)/shard_map/all_gather | solution.py:100
  127.6 130.9 %all-reduce.15.cloned.1.call-start = ((), (), s32[]{:S(2)}) async-start(), calls=%async_computation.10 | async-start | bytes 2310144 | tf_op jit(solution)/shard_map/psum | solution.py:33
  195.3 5.8 %copy-start.33 = (bf16[768,768]{1,0:T(8,128)(2,1)S(1)}, bf16[768,768]{1,0:T(8,128)(2,1)}, u32[]{:S(2)}) copy-start(bf16[768,768]{1,0:T(8,128)(2,1)} %all-gather.8.cloned.1.call-done) | copy-start | bytes 3538948
  203.2 134.7 %all-reduce.21.cloned.1.call-start = ((), (), s32[]{:S(2)}) async-start(), calls=%async_computation.20 | async-start | bytes 2359296
  269.4 26.0 %copy-start.35 = (u32[32]{0:T(128)S(1)}, u32[32]{0:T(128)}, u32[]{:S(2)}) copy-start(u32[32]{0:T(128)} %constant.141) | copy-start | bytes 388
  295.4 141.3 %all-reduce.17.cloned.1.call-start = ((), (), s32[]{:S(2)}) async-start(), calls=%async_computation.18 | async-start | bytes 4620288 | tf_op jit(solution)/shard_map/psum | solution.py:33
  296.7 44.3 %copy-start.15 = (bf16[3,1,750,64]{2,3,1,0:T(8,128)(2,1)S(1)}, bf16[3,1,750,64]{2,3,1,0:T(8,128)(2,1)}, u32[]{:S(2)}) copy-start(bf16[3,1,750,64]{2,3,1,0:T(8,128)(2,1)} %get-tuple-element.98) | copy-start | bytes 864004
  296.7 44.3 %copy-start.17 = (bf16[768,3,192]{0,2,1:T(8,128)(2,1)S(1)}, bf16[768,3,192]{0,2,1:T(8,128)(2,1)}, u32[]{:S(2)}) copy-start(bf16[768,3,192]{0,2,1:T(8,128)(2,1)} %copy.79) | copy-start | bytes 2654212
  343.2 99.4 %reduce-scatter.30.cloned.1.call-start = ((), (), s32[]{:S(2)}) async-start(), calls=%async_computation.17 | async-start | bytes 245760
  344.1 99.4 %reduce-scatter.26.cloned.1.call-start = ((), (), s32[]{:S(2)}) async-start(), calls=%async_computation.15 | async-start | bytes 491520
  348.4 96.7 %reduce-scatter.24.cloned.1.call-start = ((), (), s32[]{:S(2)}) async-start(), calls=%async_computation.14 | async-start | bytes 61440
  350.8 4.2 copy-start.32
  350.8 95.1 %reduce-scatter.22.cloned.1.call-start = ((), (), s32[]{:S(2)}) async-start(), calls=%async_computation.13 | async-start | bytes 1474560 | tf_op jit(solution)/shard_map/reduce_scatter | solution.py:236
  354.8 4.0 copy-start.16
  354.8 4.0 copy-start.24
  354.8 4.0 copy-start.26
  354.9 113.7 %reduce-scatter.20.cloned.1.call-start = ((), (), s32[]{:S(2)}) async-start(), calls=%async_computation.12 | async-start | bytes 1474560 | tf_op jit(solution)/shard_map/reduce_scatter | solution.py:230
  358.8 137.7 %reduce-scatter.18.cloned.1.call-start = ((), (), s32[]{:S(2)}) async-start(), calls=%async_computation.11 | async-start | bytes 1474560 | tf_op jit(solution)/shard_map/reduce_scatter | solution.py:218
  361.4 78.8 %copy-start.29 = (f32[750]{0:T(1024)S(1)}, f32[750]{0:T(1024)}, u32[]{:S(2)}) copy-start(f32[750]{0:T(1024)} %copy-done.28) | copy-start | bytes 9004
  361.4 157.8 %reduce-scatter.28.cloned.1.call-start = ((), (), s32[]{:S(2)}) async-start(), calls=%async_computation.16 | async-start | bytes 245760
  440.2 56.4 %copy-start.30 = (f32[768]{0:T(1024)S(1)}, f32[768]{0:T(1024)}, u32[]{:S(2)}) copy-start(f32[768]{0:T(1024)} %get-tuple-element.135) | copy-start | bytes 9220
  442.5 93.0 %all-reduce.19.cloned.1.call-start = ((), (), s32[]{:S(2)}) async-start(), calls=%async_computation.19 | async-start | bytes 1966080 | tf_op jit(solution)/shard_map/psum | solution.py:209
  (38 other events, 53.9 us)
Sparse Core Ops, SparseCore 0:
  126.6 57.0 all-reduce.12
  203.3 55.1 all-reduce.14
  295.5 42.3 all-reduce.20
  343.3 93.3 all-reduce.16
  496.7 38.7 all-reduce.18
Sparse Core Ops, SparseCore 1:
  128.5 18.6 all-gather.7
  148.6 17.3 all-gather.9
  346.1 19.7 reduce-scatter.29
  369.0 20.7 reduce-scatter.25
  392.8 19.5 reduce-scatter.23
  414.9 25.5 reduce-scatter.21
  442.9 25.5 reduce-scatter.19
  470.9 25.5 reduce-scatter.17
  499.4 19.8 reduce-scatter.27
where the time goes:
time: 552 us; the launch traced here: 550 us
  waiting for transfers between devices  295 us (53%)
  blocking collectives  82.5 us (15%)
  matrix products  67.9 us (12%)
  local copies, waits for them, and re-layouts  51 us (9%)
  other arithmetic  35.2 us (6%)
  between operations  17.4 us (3%)
    psum x3, waiting for transfers between devices, tensor_sum(): return lax.psum(partial_rows.astype(jnp.bfloat16), 'tp').astype(jnp.float32)  179 us
    unnamed x19, waiting for transfers between devices  56.6 us
    reduce_scatter x1, waiting for transfers between devices, per_device(): lax.psum_scatter(grad_tuple[0].astype(jnp.bfloat16), 'shard', scatter_dim...  28 us
    reduce_scatter x1, waiting for transfers between devices, per_device(): lax.psum_scatter(grad_tuple[4].astype(jnp.bfloat16), 'shard', scatter_dim...  22.6 us
    all_gather x1, blocking collectives, per_device(): lax.all_gather(projected[:, :, 2], 'ctx', axis=1, tiled=True)  20.3 us
    all_gather x1, blocking collectives, per_device(): lax.all_gather(projected[:, :, 1], 'ctx', axis=1, tiled=True)  19.4 us
    all_gather x1, blocking collectives, per_device(): lax.all_gather(w_qkv, 'shard', axis=0, tiled=True)  13.1 us
    unnamed x71, local copies, waits for them, and re-layouts  12.7 us
  transfers between devices with their start and end apart: 14, of which 8 were waited for; matrix products, arithmetic and copies ran while one was open for 9% of the time, Pallas kernels for 0%

commit v1 on v0

--- a/solution.py
+++ b/solution.py
@@ -2,8 +2,15 @@
 import jax.numpy as jnp
 from jax import lax
 from jax.sharding import PartitionSpec as P
+from jax.lax import all_gather
 
 HEAD_DIM = 64
+
+
+def match_block(vector, net_axis):
+    found_now = all_gather(vector, net_axis)
+    then = jnp.sum(found_now, axis=0)
+    return then
 
 
 def norm_rows(rows, gain_vec, bias_vec):
@@ -30,7 +37,7 @@
 
 
 def tensor_sum(partial_rows):
-    return lax.psum(partial_rows.astype(jnp.bfloat16), "tp").astype(jnp.float32)
+    return match_block(partial_rows.astype(jnp.bfloat16), net_axis="tp").astype(jnp.float32)
 
 
 def head_forward(operands):

time: 552 us -> 850 us (1.54)
  waiting for transfers between devices: 295 us -> 576 us
  other arithmetic: 35.2 us -> 45.5 us
    all_gather x0 -> x4, waiting for transfers between devices: none -> 338 us  [match_block(): found_now = all_gather(vector, net_axis)]
    psum x3 -> x0, waiting for transfers between devices: 179 us -> none  [tensor_sum(): return lax.psum(partial_rows.astype(jnp.bfloat16), 'tp').astype(jnp.float32)]
    unnamed x19 -> x20, waiting for transfers between devices: 56.6 us -> 91.4 us
    psum x1, waiting for transfers between devices: 8.6 us -> 40.5 us  [per_device(): lax.psum(grad_tuple[0].astype(jnp.bfloat16), 'ctx').astype(jnp.float32)]
    reduce_scatter x1, waiting for transfers between devices: 0.01 us -> 26.6 us  [per_device(): lax.psum_scatter(grad_tuple[6].astype(jnp.bfloat16), 'shard', scatter_dim...]
    all_gather x1, waiting for transfers between devices: 0.03 us -> 12.6 us  [per_device(): lax.all_gather(w_fc1, 'shard', axis=0, tiled=True)]
    all_gather x1, waiting for transfers between devices: 0.01 us -> 9.95 us  [per_device(): lax.all_gather(w_fc2, 'shard', axis=1, tiled=True)]
  transfers between devices with their start and end apart: 14 -> 15, of which waited for: 8 -> 15; matrix products, arithmetic and copies ran while one was open for 9% -> 7% of each run, Pallas kernels for 0% -> 0%
where the time goes in v1:
time: 850 us; the launch traced here: 842 us
  waiting for transfers between devices  576 us (68%)
  blocking collectives  82.5 us (10%)
  matrix products  69.2 us (8%)
  local copies, waits for them, and re-layouts  50.9 us (6%)
  other arithmetic  45.5 us (5%)
  between operations  16 us (2%)
    all_gather x4, waiting for transfers between devices, match_block(): found_now = all_gather(vector, net_axis)  338 us
    unnamed x20, waiting for transfers between devices  91.4 us
    psum x1, waiting for transfers between devices, per_device(): lax.psum(grad_tuple[0].astype(jnp.bfloat16), 'ctx').astype(jnp.float32)  40.5 us
    reduce_scatter x1, waiting for transfers between devices, per_device(): lax.psum_scatter(grad_tuple[0].astype(jnp.bfloat16), 'shard', scatter_dim...  28.2 us
    reduce_scatter x1, waiting for transfers between devices, per_device(): lax.psum_scatter(grad_tuple[4].astype(jnp.bfloat16), 'shard', scatter_dim...  28.2 us
    reduce_scatter x1, waiting for transfers between devices, per_device(): lax.psum_scatter(grad_tuple[6].astype(jnp.bfloat16), 'shard', scatter_dim...  26.6 us
    all_gather x1, blocking collectives, per_device(): lax.all_gather(projected[:, :, 2], 'ctx', axis=1, tiled=True)  20.3 us
    all_gather x1, blocking collectives, per_device(): lax.all_gather(projected[:, :, 1], 'ctx', axis=1, tiled=True)  19.4 us
  transfers between devices with their start and end apart: 15, of which 15 were waited for; matrix products, arithmetic and copies ran while one was open for 7% of the time, Pallas kernels for 0%

profile of v1, /device:TPU:0, one launch (start us, length us, event | category | flops | bytes accessed | tf_op | source)
XLA Modules:
  0.0 841.5 jit_solution(2383244722688818706)
XLA Ops:
  11.3 6.2 all-gather.8
  20.9 5.5 all-gather.7
  27.2 7.1 all_gather.60
  34.5 13.1 %all_gather.56 = bf16[768,3,192]{2,1,0:T(4,128)(2,1)S(1)} all-gather(bf16[192,3,192]{2,1,0:T(4,128)(2,1)S(1)} %copy.78), channel_id=1, replica_groups=mesh['shard'=4,'ctx'=2,'tp'=4] {'shard'}, dimensions={0}, use_global_device_ids=true | all-gather | bytes 1105920 | tf_op jit(solution)/shard_map/all_gather | solution.py:101
  55.1 20.3 %all-gather.1 = bf16[1,1500,1,192]{3,2,0,1:T(2,128)(2,1)S(1)} all-gather(bf16[1,750,1,192]{3,2,0,1:T(2,128)(2,1)} %copy.84), channel_id=3, replica_groups=mesh['shard'=4,'ctx'=2,'tp'=4] {'ctx'}, dimensions={1}, use_global_device_ids=true | all-gather | bytes 864000 | tf_op jit(solution)/shard_map/all_gather | solution.py:128
  83.6 19.4 %all-gather = bf16[1,1500,1,192]{3,2,0,1:T(2,128)(2,1)S(1)} all-gather(bf16[1,750,1,192]{3,2,0,1:T(2,128)(2,1)} %copy.82), channel_id=2, replica_groups=mesh['shard'=4,'ctx'=2,'tp'=4] {'ctx'}, dimensions={1}, use_global_device_ids=true | all-gather | bytes 864000 | tf_op jit(solution)/shard_map/all_gather | solution.py:127
  108.5 14.4 %while.26 = (s32[]{:T(128)}, bf16[3,1,750,64]{2,3,1,0:T(8,128)(2,1)}, f32[3,1,750]{2,1,0:T(1,128)S(1)}, bf16[3,1,750,64]{3,2,1,0:T(8,128)(2,1)S(1)}, bf16[3,1,15...) while((s32[]{:T(128)}, bf16[3,1,750,64]{2,3,1,0:T(8,128)(2,1)}, ...), condition=%wide.region_5.6_spmd, body=%wide.region_2.5_spmd.sunk | while | flops 298124256 | bytes 17119008 | solution.py:133
  128.7 5.9 all-reduce
  134.6 80.3 %all-gather.24.cloned.1.call-done = bf16[4,750,768]{2,1,0:T(8,128)(2,1)} async-done(((bf16[1,750,768]{2,1,0:T(8,128)(2,1)}), bf16[4,750,768]{2,1,0:T(8,128)(2,1)}) %all-gather.24.cloned.1.call-update) | async-done | bytes 4608016 | tf_op jit(solution)/shard_map/all_gather | solution.py:11
  219.8 12.6 %all-gather.20.cloned.1.call-done = bf16[768,768]{1,0:T(8,128)(2,1)} async-done(((bf16[192,768]{1,0:T(8,128)(2,1)}), bf16[768,768]{1,0:T(8,128)(2,1)}) %all-gather.20.cloned.1.call-update) | async-done | bytes 1179664 | tf_op jit(solution)/shard_map/all_gather | solution.py:105
  232.4 9.1 %multiply_convert_fusion.1 = (bf16[750,768]{1,0:T(8,128)(2,1)}, f32[750,768]{1,0:T(8,128)}, f32[750,768]{1,0:T(8,128)}) fusion(f32[768]{0:T(1024)S(1)} %convert_element_type.361, bf16[768,768]{1,0:T(8,128)(2,1)} %all-gather.20.cloned.1.call-done, f32[768]{0:T(1024)S(1)} %get-tuple-element.140, f32[768]{0:T(1024)S(1)} %get-tuple-element.141, ...), kind=kOutput, calls=%fused_computation.86 | convolution fusion | flops 927936000 | bytes 9261936 | tf_op jit(solution)/shard_map/cfd,dh->cfh/dot_general | solution.py:139
  241.4 9.9 %all-gather.22.cloned.1.call-done = bf16[768,768]{0,1:T(8,128)(2,1)} async-done(((bf16[768,192]{0,1:T(8,128)(2,1)}), bf16[768,768]{0,1:T(8,128)(2,1)}) %all-gather.22.cloned.1.call-update) | async-done | bytes 1179664 | tf_op jit(solution)/shard_map/all_gather | solution.py:107
  251.4 4.8 fusion.102
  260.0 87.3 %all-gather.28.cloned.1.call-done = bf16[4,750,768]{2,1,0:T(8,128)(2,1)} async-done(((bf16[1,750,768]{2,1,0:T(8,128)(2,1)}), bf16[4,750,768]{2,1,0:T(8,128)(2,1)}) %all-gather.28.cloned.1.call-update) | async-done | bytes 4608016 | tf_op jit(solution)/shard_map/all_gather | solution.py:11
  347.3 4.6 fusion.95
  361.3 25.9 %while.27 = (s32[]{:T(128)}, bf16[3,1,750,64]{2,3,1,0:T(8,128)(2,1)}, bf16[3,1,1500,64]{2,3,1,0:T(8,128)(2,1)}, bf16[3,1,1500,64]{2,3,1,0:T(8,128)(2,1)}, bf16[3...) while((s32[]{:T(128)}, ...), condition=%wide.region_15.16_spmd, body=%wide.region_13.15_spmd.sunk | while | flops 729143232 | bytes 49712548 | solution.py:176
  395.5 3.8 convolution_convert_fusion.1
  400.6 28.2 %all-reduce.11.cloned.1.call-done = (bf16[1,1500,192]{1,2,0:T(8,128)(2,1)}, bf16[1,1500,192]{1,2,0:T(8,128)(2,1)}) async-done(((bf16[1,1500,192]{1,2,0:T(8,128)(2,1)}, bf16[1,1500,192]{1,2,0:T(8,128)(2,1)}), (bf16[1,1500,192]{1,2,0:T(8,128)(2,1)}, bf16[1,1500,192]{1,2,0:T(8,128)(2,1)})) %all-reduce.11.cloned.1.call-update) | async-done | bytes 1152016
  439.3 13.3 %reduce-scatter.26.cloned.1.call-done = bf16[192,192]{1,0:T(8,128)(2,1)} async-done(((bf16[768,192]{1,0:T(8,128)(2,1)}), bf16[192,192]{1,0:T(8,128)(2,1)}) %reduce-scatter.26.cloned.1.call-update) | async-done | bytes 73744
  454.2 26.6 %reduce-scatter.22.cloned.1.call-done = bf16[768,192]{0,1:T(8,128)(2,1)} async-done(((bf16[768,768]{0,1:T(8,128)(2,1)}), bf16[768,192]{0,1:T(8,128)(2,1)}) %reduce-scatter.22.cloned.1.call-update) | async-done | bytes 294928 | tf_op jit(solution)/shard_map/reduce_scatter | solution.py:243
  480.8 28.2 %reduce-scatter.20.cloned.1.call-done = bf16[192,768]{1,0:T(8,128)(2,1)} async-done(((bf16[768,768]{1,0:T(8,128)(2,1)}), bf16[192,768]{1,0:T(8,128)(2,1)}) %reduce-scatter.20.cloned.1.call-update) | async-done | bytes 294928 | tf_op jit(solution)/shard_map/reduce_scatter | solution.py:237
  509.0 28.2 %reduce-scatter.18.cloned.1.call-done = bf16[192,3,192]{2,0,1:T(8,128)(2,1)} async-done(((bf16[768,3,192]{2,0,1:T(8,128)(2,1)}), bf16[192,3,192]{2,0,1:T(8,128)(2,1)}) %reduce-scatter.18.cloned.1.call-update) | async-done | bytes 221200 | tf_op jit(solution)/shard_map/reduce_scatter | solution.py:225
  540.9 18.9 %reduce-scatter.30.cloned.1.call-done = bf16[192,1]{1,0:T(8,128)(2,1)} async-done(((bf16[768,1]{1,0:T(8,128)(2,1)}), bf16[192,1]{1,0:T(8,128)(2,1)}) %reduce-scatter.30.cloned.1.call-update) | async-done | bytes 400
  561.3 87.9 %all-gather.26.cloned.1.call-done = bf16[4,750,768]{2,1,0:T(8,128)(2,1)} async-done(((bf16[1,750,768]{2,1,0:T(8,128)(2,1)}), bf16[4,750,768]{2,1,0:T(8,128)(2,1)}) %all-gather.26.cloned.1.call-update) | async-done | bytes 4608016 | tf_op jit(solution)/shard_map/all_gather | solution.py:11
  649.2 4.4 reduce.39
  653.6 15.9 %reduce-scatter.24.cloned.1.call-done = bf16[48,2]{1,0:T(8,128)(2,1)} async-done(((bf16[192,2]{1,0:T(8,128)(2,1)}), bf16[48,2]{1,0:T(8,128)(2,1)}) %reduce-scatter.24.cloned.1.call-update) | async-done | bytes 208
  670.8 40.5 %all-reduce.9.cloned.1.call-done = (bf16[192,3,192]{2,0,1:T(8,128)(2,1)}, bf16[192,192]{1,0:T(8,128)(2,1)}, bf16[192,768]{1,0:T(8,128)(2,1)}, bf16[768,192]{0,1:T(8,128)(2,1)}) async-done(((bf16[192,3,192]{2,0,1:T(8,128)(2,1)}, bf16[192,192]{1,0:T(8,128)(2,1)}, bf16[192,768]{1,0:T(8,128)(2,1)}, bf16[768,192]{0,1:T(8,128)(2,1)}), (bf16[192,3,192]{2,0,1:T(8,128)(2,1)}, bf16[192,192]{1,0:T(8,128)(2,1)}, ...) | async-done | bytes 884752 | tf_op jit(solution)/shard_map/psum | solution.py:216
  718.3 82.8 %all-gather.30.cloned.1.call-done = bf16[4,750,768]{2,1,0:T(8,128)(2,1)} async-done(((bf16[1,750,768]{2,1,0:T(8,128)(2,1)}), bf16[4,750,768]{2,1,0:T(8,128)(2,1)}) %all-gather.30.cloned.1.call-update) | async-done | bytes 4608016 | tf_op jit(solution)/shard_map/all_gather | solution.py:11
  801.1 4.6 fusion.96
  808.8 4.8 add_convert_fusion
  813.6 13.5 %reduce-scatter.28.cloned.1.call-done = bf16[192,6]{1,0:T(8,128)(2,1)} async-done(((bf16[768,6]{1,0:T(8,128)(2,1)}), bf16[192,6]{1,0:T(8,128)(2,1)}) %reduce-scatter.28.cloned.1.call-update) | async-done | bytes 2320
  828.0 5.0 all-reduce.3
  (259 shorter events, 132.6 us)
Async XLA Ops:
  7.2 19.9 %copy-start.22 = (bf16[192,192]{1,0:T(8,128)(2,1)S(1)}, bf16[192,192]{1,0:T(8,128)(2,1)}, u32[]{:S(2)}) copy-start(bf16[192,192]{1,0:T(8,128)(2,1)} %param.21) | copy-start | bytes 221188
  7.2 27.1 %copy-start.20 = (bf16[192,3,192]{2,0,1:T(8,128)(2,1)S(1)}, bf16[192,3,192]{2,0,1:T(8,128)(2,1)}, u32[]{:S(2)}) copy-start(bf16[192,3,192]{2,0,1:T(8,128)(2,1)} %param.19) | copy-start | bytes 663556
  7.2 207.7 %all-gather.24.cloned.1.call-start = ((), (), s32[]{:S(2)}) async-start(), calls=%async_computation.12 | async-start | bytes 5775360 | tf_op jit(solution)/shard_map/all_gather | solution.py:11
  20.8 5.5 copy-start.23
  34.5 15.3 %copy-start = (bf16[1,750,768]{2,1,0:T(8,128)(2,1)S(1)}, bf16[1,750,768]{2,1,0:T(8,128)(2,1)}, u32[]{:S(2)}) copy-start(bf16[1,750,768]{2,1,0:T(8,128)(2,1)} %param.18) | copy-start | bytes 3456004
  108.5 14.4 %copy-start.9 = (bf16[192,768]{0,1:T(8,128)(2,1)S(1)}, bf16[192,768]{0,1:T(8,128)(2,1)}, u32[]{:S(2)}) copy-start(bf16[192,768]{0,1:T(8,128)(2,1)} %all_gather.60) | copy-start | bytes 884740
  122.9 11.7 %copy-start.3 = (bf16[3,1,750,64]{3,2,1,0:T(8,128)(2,1)}, bf16[3,1,750,64]{3,2,1,0:T(8,128)(2,1)S(1)}, u32[]{:S(2)}) copy-start(bf16[3,1,750,64]{3,2,1,0:T(8,128)(2,1)S(1)} %get-tuple-element.394) | copy-start | bytes 864004
  122.9 4.3 copy-start.31
  122.9 5.6 copy-start.29
  125.7 106.7 %all-gather.20.cloned.1.call-start = ((), (), s32[]{:S(2)}) async-start(), calls=%async_computation.7 | async-start | bytes 1474560 | tf_op jit(solution)/shard_map/all_gather | solution.py:105
  126.4 125.0 %all-gather.22.cloned.1.call-start = ((), (), s32[]{:S(2)}) async-start(), calls=%async_computation.8 | async-start | bytes 1474560 | tf_op jit(solution)/shard_map/all_gather | solution.py:107
  127.1 220.2 %all-gather.28.cloned.1.call-start = ((), (), s32[]{:S(2)}) async-start(), calls=%async_computation.14 | async-start | bytes 5775360 | tf_op jit(solution)/shard_map/all_gather | solution.py:11
  251.4 5.9 copy-start.28
  259.4 169.4 %all-reduce.11.cloned.1.call-start = ((), (), s32[]{:S(2)}) async-start(), calls=%async_computation.21 | async-start | bytes 2359296
  354.5 2.7 copy-start.10
  387.2 4.6 copy-start.8
  387.3 65.3 %reduce-scatter.26.cloned.1.call-start = ((), (), s32[]{:S(2)}) async-start(), calls=%async_computation.17 | async-start | bytes 491520
  391.8 89.0 %reduce-scatter.22.cloned.1.call-start = ((), (), s32[]{:S(2)}) async-start(), calls=%async_computation.11 | async-start | bytes 1474560 | tf_op jit(solution)/shard_map/reduce_scatter | solution.py:243
  395.3 4.1 copy-start.30
  395.3 113.7 %reduce-scatter.20.cloned.1.call-start = ((), (), s32[]{:S(2)}) async-start(), calls=%async_computation.10 | async-start | bytes 1474560 | tf_op jit(solution)/shard_map/reduce_scatter | solution.py:237
  399.3 31.6 %copy-start.15 = (bf16[3,1,750,64]{2,3,1,0:T(8,128)(2,1)S(1)}, bf16[3,1,750,64]{2,3,1,0:T(8,128)(2,1)}, u32[]{:S(2)}) copy-start(bf16[3,1,750,64]{2,3,1,0:T(8,128)(2,1)} %get-tuple-element.98) | copy-start | bytes 864004
  399.3 137.9 %reduce-scatter.18.cloned.1.call-start = ((), (), s32[]{:S(2)}) async-start(), calls=%async_computation.9 | async-start | bytes 1474560 | tf_op jit(solution)/shard_map/reduce_scatter | solution.py:225
  433.4 126.4 %reduce-scatter.30.cloned.1.call-start = ((), (), s32[]{:S(2)}) async-start(), calls=%async_computation.19 | async-start | bytes 245760
  434.4 214.9 %all-gather.26.cloned.1.call-start = ((), (), s32[]{:S(2)}) async-start(), calls=%async_computation.13 | async-start | bytes 5775360 | tf_op jit(solution)/shard_map/all_gather | solution.py:11
  438.2 231.3 %reduce-scatter.24.cloned.1.call-start = ((), (), s32[]{:S(2)}) async-start(), calls=%async_computation.16 | async-start | bytes 61440
  439.2 272.0 %all-reduce.9.cloned.1.call-start = ((), (), s32[]{:S(2)}) async-start(), calls=%async_computation.20 | async-start | bytes 1966080 | tf_op jit(solution)/shard_map/psum | solution.py:216
  537.2 263.9 %all-gather.30.cloned.1.call-start = ((), (), s32[]{:S(2)}) async-start(), calls=%async_computation.15 | async-start | bytes 5775360 | tf_op jit(solution)/shard_map/all_gather | solution.py:11
  540.7 286.5 %reduce-scatter.28.cloned.1.call-start = ((), (), s32[]{:S(2)}) async-start(), calls=%async_computation.18 | async-start | bytes 245760
  805.8 3.0 copy-start.2
  805.8 3.0 copy-start.25
  808.8 19.2 %copy-start.26 = (bf16[192,1]{0,1:T(2,128)(2,1)S(1)}, bf16[192,1]{0,1:T(2,128)(2,1)}, u32[]{:S(2)}) copy-start(bf16[192,1]{0,1:T(2,128)(2,1)} %copy.104) | copy-start | bytes 1156
  808.8 19.2 %copy-start.27 = (bf16[48,2]{0,1:T(2,128)(2,1)S(1)}, bf16[48,2]{0,1:T(2,128)(2,1)}, u32[]{:S(2)}) copy-start(bf16[48,2]{0,1:T(2,128)(2,1)} %copy.98) | copy-start | bytes 580
  (34 other events, 42.6 us)
Sparse Core Ops, SparseCore 0:
  125.8 89.0 all-gather.23
  216.5 15.8 all-gather.19
  233.9 17.4 all-gather.21
  259.5 87.7 all-gather.27
  387.4 41.3 all-reduce.10
  431.7 20.8 reduce-scatter.25
  455.1 25.6 reduce-scatter.21
  483.4 25.5 reduce-scatter.19
  511.6 25.5 reduce-scatter.17
  540.0 19.7 reduce-scatter.29
  561.4 87.7 all-gather.25
  651.5 17.9 reduce-scatter.23
  672.5 38.6 all-reduce.8
  713.3 87.7 all-gather.29
  808.9 18.2 reduce-scatter.27
